TPU v7x, 32 devices: a whole 2x2x4 slice. The times are simulated.
32 devices in a mesh: wide: 8 (over z, y), narrow: 4 (over x, core).
Axes of the slice: x: 2, y: 2, z: 4, core: 2. Of those that a mesh axis runs over, the one named last changes fastest.
Arguments:
- residual: float32 [8, 4, 6, 192, 512], P('wide', 'narrow'), may hold values from -6 to 6
- face_schur: float32 [8, 4, 6, 192, 192], P('wide', 'narrow'), may hold values from -0.5 to 1.5, as said below
- local_solver: bfloat16 [8, 4, 1152, 1152], P('wide', 'narrow'), may hold values from -0.1875 to 0.1875
- interface_functional_set: float32 [3, 192, 16], replicated, may hold values from -0.4375 to 0.4375
- coarse_inverse: float32 [1536, 1536], P('wide', 'narrow'), may hold values from -0.3125 to 0.3125
Outputs:
- preconditioned: float32 [8, 4, 3, 192, 512], P('wide', 'narrow')
Inputs may be any that keep to these rules, and one draw needn't show every extreme that they name: `face_schur`: every face block is symmetric positive definite.
All inputs are finite; a program needn't handle non-finite values. Where the computation divides by a largest or mean magnitude, that divisor is 1e-20 or more.
Results may differ from a plain program's by a relative error of at most 0.002.
Values sent between devices are 32-bit elements; how exact they have to be, the bound alone decides.
No kernel may reach another device: no remote copies, remote signals or barrier semaphores. Data moves between devices by JAX's collectives and lax.ppermute only.
A program may use at most 64 MiB of HBM per device.

v0:
```python
import jax
import jax.numpy as jnp
from jax import lax
from jax.sharding import PartitionSpec as P

NS_STEPS = 12
exact_arithmetic_mode = lax.Precision.HIGHEST


def passed_along(value, axis, steps):
    count = lax.axis_size(axis)
    pairs = [(source, (source + steps) % count) for source in range(count)]
    return lax.ppermute(value, axis, pairs)


def newton_schulz(matrices):
    row_sums = jnp.max(jnp.sum(jnp.abs(matrices), axis=2), axis=1)
    approx = matrices / (row_sums * row_sums)[:, None, None]
    for iteration in range(NS_STEPS):
        product = jnp.einsum("bij,bjk->bik", matrices, approx, precision=exact_arithmetic_mode)
        approx = 2.0 * approx - jnp.einsum(
            "bij,bjk->bik", approx, product, precision=exact_arithmetic_mode
        )
    return approx


def apply_faces(blocks, fields):
    return jnp.einsum("fij,fjr->fir", blocks, fields, precision=exact_arithmetic_mode)


def per_device(residual, face_schur, local_solver, interface_functional_set, coarse_inverse):
    blocks = face_schur[0, 0]
    face_loads = residual[0, 0]
    face_order = blocks.shape[1]
    columns_count = face_loads.shape[2]
    wide_low = jnp.concatenate([blocks[0], face_loads[0]], axis=1)
    wide_above = passed_along(wide_low, "wide", -1)
    narrow_low = jnp.concatenate([blocks[2], face_loads[2]], axis=1)
    narrow_above = passed_along(narrow_low, "narrow", -1)
    owned_sums = jnp.stack(
        [
            blocks[1] + wide_above[:, :face_order],
            blocks[3] + narrow_above[:, :face_order],
            blocks[4] + blocks[5],
        ],
        axis=0,
    )
    owned_values = jnp.stack(
        [
            face_loads[1] + wide_above[:, face_order:],
            face_loads[3] + narrow_above[:, face_order:],
            face_loads[4] + face_loads[5],
        ],
        axis=0,
    )
    owned_inverse = newton_schulz(owned_sums)
    owned_scaled = apply_faces(owned_inverse, owned_values)
    wide_below = passed_along(owned_scaled[0], "wide", 1)
    narrow_below = passed_along(owned_scaled[1], "narrow", 1)
    face_scaled = jnp.stack(
        [
            wide_below,
            owned_scaled[0],
            narrow_below,
            owned_scaled[1],
            owned_scaled[2],
            owned_scaled[2],
        ],
        axis=0,
    )
    restricted_residual = jnp.einsum(
        "psk,pse->pke", interface_functional_set, owned_values, precision=exact_arithmetic_mode
    )
    restricted_residual = restricted_residual.reshape(-1, columns_count)
    incomplete_total = jnp.dot(
        coarse_inverse,
        lax.all_gather(restricted_residual, "wide", axis=0, tiled=True),
        precision=exact_arithmetic_mode,
        preferred_element_type=jnp.float32,
    )
    own_rows = restricted_residual.shape[0]
    summed = lax.psum(incomplete_total, "narrow")
    own_coarse = lax.dynamic_slice_in_dim(summed, lax.axis_index("narrow") * own_rows, own_rows, 0)
    local_loads = apply_faces(blocks, face_scaled).astype(jnp.bfloat16)
    flattened = local_loads.reshape(-1, columns_count)
    solved = jnp.dot(local_solver[0, 0], flattened, preferred_element_type=jnp.float32)
    solved = solved.reshape(6, face_order, columns_count)
    weighted = apply_faces(blocks, solved)
    wide_back = passed_along(weighted[0], "wide", -1)
    narrow_back = passed_along(weighted[2], "narrow", -1)
    combined = jnp.stack(
        [weighted[1] + wide_back, weighted[3] + narrow_back, weighted[4] + weighted[5]], axis=0
    )
    local_part = apply_faces(owned_inverse, combined)
    update_increment = own_coarse.reshape(3, -1, columns_count)
    coarse_component = jnp.einsum(
        "fek,fkg->feg", interface_functional_set, update_increment, precision=exact_arithmetic_mode
    )
    output_answer = local_part + coarse_component
    return output_answer[None, None]


def solution(mesh):
    placed = (
        P("wide", "narrow", None, None, None),
        P("wide", "narrow", None, None, None),
        P("wide", "narrow", None, None),
        P(),
        P("wide", "narrow"),
    )
    return jax.shard_map(
        per_device,
        mesh=mesh,
        in_specs=placed,
        out_specs=P("wide", "narrow", None, None, None),
        check_vma=False,
    )
```

profile of v0, /device:TPU:0, one launch (start us, length us, event | category | flops | bytes accessed | tf_op | source)
XLA Modules:
  0.0 147.2 jit_solution(12711466252790806071)
XLA Ops:
  6.5 1.4 add_bitcast_fusion.1
  8.0 2.3 %slice_bitcast_fusion.6 = (f32[192,512]{1,0:T(8,128)S(1)}, f32[192,512]{1,0:T(8,128)S(1)}, f32[1,192,512]{2,1,0:T(8,128)}) fusion(f32[1,1,6,192,512]{4,3,2,1,0:T(8,128)} %param.5), kind=kLoop, calls=%fused_computation.57 | loop fusion | flops 98304 | bytes 2752512 | tf_op jit(solution)/shard_map/squeeze | solution.py:36
  10.4 2.5 %collective-permute-start.1 = (f32[192,704]{1,0:T(8,128)S(1)}, f32[192,704]{1,0:T(8,128)S(1)}, u32[]{:S(2)}, u32[]{:S(2)}) collective-permute-start(f32[192,704]{1,0:T(8,128)S(1)} %pad_maximum_fusion.4), channel_id=1, source_target_pairs={{0,3},{1,0},{2,1},{3,2},{4,7},{5,4},{6,5},{7,6},{8,11},{9,8},{10,9... | collective-permute-start | bytes 1622024 | tf_op jit(solution)/shard_map/ppermute | solution.py:13
  13.1 4.6 %collective-permute-start = (f32[192,704]{1,0:T(8,128)S(1)}, f32[192,704]{1,0:T(8,128)S(1)}, u32[]{:S(2)}, u32[]{:S(2)}) collective-permute-start(f32[192,704]{1,0:T(8,128)S(1)} %pad_maximum_fusion.3), channel_id=1, source_target_pairs={{0,28},{4,0},{8,4},{12,8},{16,12},{20,16},{24,20},{28,24},{1,29},{... | collective-permute-start | bytes 1622024 | tf_op jit(solution)/shard_map/ppermute | solution.py:13
  17.7 2.6 %collective-permute-done.1 = f32[192,704]{1,0:T(8,128)S(1)} collective-permute-done((f32[192,704]{1,0:T(8,128)S(1)}, f32[192,704]{1,0:T(8,128)S(1)}, u32[]{:S(2)}, u32[]{:S(2)}) %collective-permute-start.1) | collective-permute-done | bytes 540704 | tf_op jit(solution)/shard_map/ppermute | solution.py:13
  20.3 9.7 %collective-permute-done = f32[192,704]{1,0:T(8,128)S(1)} collective-permute-done((f32[192,704]{1,0:T(8,128)S(1)}, f32[192,704]{1,0:T(8,128)S(1)}, u32[]{:S(2)}, u32[]{:S(2)}) %collective-permute-start) | collective-permute-done | bytes 540704 | tf_op jit(solution)/shard_map/ppermute | solution.py:13
  30.0 1.3 fusion.23
  31.6 0.8 fusion.11
  32.4 0.8 convolution_subtract_fusion.11
  33.2 0.7 fusion.37
  43.4 0.9 fusion.30
  49.9 1.4 fusion.19
  51.3 1.2 fusion.10
  53.6 12.1 %collective-permute-done.2 = f32[192,512]{1,0:T(8,128)S(1)} collective-permute-done((f32[192,512]{1,0:T(8,128)S(1)}, f32[192,512]{1,0:T(8,128)S(1)}, u32[]{:S(2)}, u32[]{:S(2)}) %collective-permute-start.2) | collective-permute-done | bytes 393248 | tf_op jit(solution)/shard_map/ppermute | solution.py:13
  65.8 0.8 slice_bitcast_fusion.4
  66.6 1.4 copy-done.4
  68.0 32.6 %all_gather.3 = f32[384,512]{1,0:T(8,128)S(1)} all-gather(f32[48,512]{1,0:T(8,128)S(1)} %bitcast.129), channel_id=1, replica_groups=mesh['wide'=8,'narrow'=4] {'wide'}, dimensions={0}, use_global_device_ids=true | all-gather | bytes 884736 | tf_op jit(solution)/shard_map/all_gather | solution.py:77
  100.6 1.6 %convolution_bitcast_fusion.3 = f32[192,512]{1,0:T(8,128)} fusion(f32[384,512]{1,0:T(8,128)S(1)} %all_gather.3, f32[192,384]{1,0:T(8,128)S(1)} %copy-done.11), kind=kOutput, calls=%fused_computation.19 | convolution fusion | flops 452984832 | bytes 1474560 | tf_op jit(solution)/shard_map/dot_general | solution.py:75
  102.3 1.8 %bitcast_dynamic-update-slice_fusion = f32[6,192,512]{2,1,0:T(8,128)} fusion(f32[6,192,512]{2,1,0:T(8,128)} %copy-done.4, f32[192,512]{1,0:T(8,128)} %collective-permute-done.3), kind=kLoop, calls=%fused_computation.53 | loop fusion | bytes 786432
  104.1 2.2 %slice_dynamic-update-slice_fusion = f32[6,192,512]{2,1,0:T(8,128)} fusion(f32[6,192,512]{2,1,0:T(8,128)} %bitcast_dynamic-update-slice_fusion, f32[3,192,512]{2,1,0:T(8,128)} %copy-done.1), kind=kLoop, calls=%fused_computation.30 | loop fusion | bytes 1572864
  106.2 1.8 %slice_dynamic-update-slice_fusion.1 = f32[6,192,512]{2,1,0:T(8,128)} fusion(f32[6,192,512]{2,1,0:T(8,128)} %slice_dynamic-update-slice_fusion, f32[3,192,512]{2,1,0:T(8,128)} %copy-done.1), kind=kLoop, calls=%fused_computation.47 | loop fusion | bytes 786432 | tf_op jit(solution)/shard_map/stack | solution.py:60
  108.0 4.0 %convolution_convert_fusion = bf16[6,512,192]{1,2,0:T(8,128)(2,1)S(1)} fusion(f32[6,192,512]{2,1,0:T(8,128)} %slice_dynamic-update-slice_fusion.1, f32[1,1,6,192,192]{4,3,2,1,0:T(8,128)S(1)} %copy-done.2), kind=kOutput, calls=%fused_computation.3 | convolution fusion | flops 1359544320 | bytes 4423680 | tf_op jit(solution)/shard_map/fij,fjr->fir/dot_general | solution.py:28
  112.0 3.4 %convolution_bitcast_fusion = f32[1152,512]{0,1:T(8,128)} fusion(bf16[1152,512]{1,0:T(8,128)(2,1)S(1)} %bitcast.127, bf16[1,1,1152,1152]{3,2,1,0:T(8,128)(2,1)S(1)} %copy-done), kind=kOutput, calls=%fused_computation | convolution fusion | flops 1358954496 | bytes 6193152 | tf_op jit(solution)/shard_map/dot_general | solution.py:86
  115.4 3.1 %copy.8 = f32[1152,512]{1,0:T(8,128)} copy(f32[1152,512]{0,1:T(8,128)} %convolution_bitcast_fusion) | data formatting | bytes 4718592 | tf_op jit(solution)/shard_map/dot_general | solution.py:86
  118.5 4.3 %convolution_bitcast_fusion.1 = f32[6,192,512]{2,1,0:T(8,128)S(1)} fusion(f32[6,192,512]{2,1,0:T(8,128)} %bitcast.126, f32[1,1,6,192,192]{4,3,2,1,0:T(8,128)} %param.6), kind=kOutput, calls=%fused_computation.2 | convolution fusion | flops 1358954496 | bytes 5603328 | tf_op jit(solution)/shard_map/fij,fjr->fir/dot_general | solution.py:28
  122.8 1.1 slice_bitcast_fusion.2
  124.6 1.4 collective-permute-start.4
  126.0 8.5 %all-reduce.2.cloned.1.call-done = f32[192,512]{1,0:T(8,128)} async-done(((f32[192,512]{1,0:T(8,128)}), f32[192,512]{1,0:T(8,128)}) %all-reduce.2.cloned.1.call-update) | async-done | bytes 393232 | tf_op jit(solution)/shard_map/psum | solution.py:82
  134.5 0.9 constant_dynamic-slice_fusion
  135.4 1.1 convolution_bitcast_fusion.2
  136.6 1.5 %fusion.17 = (f32[1,192,512]{2,1,0:T(8,128)S(1)}, f32[1,192,512]{2,1,0:T(8,128)S(1)}) fusion(f32[192,512]{1,0:T(8,128)} %collective-permute-done.4, f32[6,192,512]{2,1,0:T(8,128)} %copy-done.3, f32[192,512]{1,0:T(8,128)} %collective-permute-done.5), kind=kLoop, calls=%fused_computation.46 | loop fusion | flops 196608 | bytes 2359296 | tf_op jit(solution)/shard_map/stack | solution.py:91
  138.1 2.2 %fusion.1 = f32[1,1,3,192,512]{4,3,2,1,0:T(8,128)} fusion(f32[3,192,512]{2,1,0:T(8,128)S(1)} %convolution_bitcast_fusion.2, f32[3,192,192]{2,1,0:T(8,128)S(1)} %convolution_subtract_fusion, f32[1,192,512]{2,1,0:T(8,128)S(1)} %copy-done.6, f32[1,192,512]{2,1,0:T(8,128)S(1)} %get-tuple-element.6, f32[1,192,512]{2,1,0:T(8,128)S(1)} %get-tuple-element.5), kind=kOutput, calls=%fused_computation.6 | convolution fusion | flops 680361984 | bytes 3981312 | tf_op jit(solution)/shard_map/fij,fjr->fir/dot_general | solution.py:28
  (61 shorter events, 17.4 us)
Async XLA Ops:
  6.5 105.5 %copy-start = (bf16[1,1,1152,1152]{3,2,1,0:T(8,128)(2,1)S(1)}, bf16[1,1,1152,1152]{3,2,1,0:T(8,128)(2,1)}, u32[]{:S(2)}) copy-start(bf16[1,1,1152,1152]{3,2,1,0:T(8,128)(2,1)} %param.7) | copy-start | bytes 7962628
  6.5 128.0 %all-reduce.2.cloned.1.call-start = ((), (), s32[]{:S(2)}) async-start(), calls=%async_computation | async-start | bytes 786432 | tf_op jit(solution)/shard_map/psum | solution.py:82
  10.4 9.9 %collective-permute-start.1 = (f32[192,704]{1,0:T(8,128)S(1)}, f32[192,704]{1,0:T(8,128)S(1)}, u32[]{:S(2)}, u32[]{:S(2)}) collective-permute-start(f32[192,704]{1,0:T(8,128)S(1)} %pad_maximum_fusion.4), channel_id=1, source_target_pairs={{0,3},{1,0},{2,1},{3,2},{4,7},{5,4},{6,5},{7,6},{8,11},{9,8},{10,9... | collective-permute-start | bytes 1622024 | tf_op jit(solution)/shard_map/ppermute | solution.py:13
  13.1 16.9 %collective-permute-start = (f32[192,704]{1,0:T(8,128)S(1)}, f32[192,704]{1,0:T(8,128)S(1)}, u32[]{:S(2)}, u32[]{:S(2)}) collective-permute-start(f32[192,704]{1,0:T(8,128)S(1)} %pad_maximum_fusion.3), channel_id=1, source_target_pairs={{0,28},{4,0},{8,4},{12,8},{16,12},{20,16},{24,20},{28,24},{1,29},{... | collective-permute-start | bytes 1622024 | tf_op jit(solution)/shard_map/ppermute | solution.py:13
  20.3 9.7 %copy-start.7 = (f32[192,704]{1,0:T(8,128)}, f32[192,704]{1,0:T(8,128)S(1)}, u32[]{:S(2)}) copy-start(f32[192,704]{1,0:T(8,128)S(1)} %collective-permute-done.1) | copy-start | bytes 1622020
  30.0 1.3 copy-start.9
  48.6 1.1 copy-start.8
  48.6 1.2 copy-start.10
  49.9 1.4 copy-start.5
  51.3 1.6 %copy-start.12 = (f32[3,192,16]{1,2,0:T(8,128)S(1)}, f32[3,192,16]{1,2,0:T(8,128)}, u32[]{:S(2)}) copy-start(f32[3,192,16]{1,2,0:T(8,128)} %param.8) | copy-start | bytes 110596
  52.5 13.3 %copy-start.1 = (f32[3,192,512]{2,1,0:T(8,128)}, f32[3,192,512]{2,1,0:T(8,128)S(1)}, u32[]{:S(2)}) copy-start(f32[3,192,512]{2,1,0:T(8,128)S(1)} %fusion.10) | copy-start | bytes 3538948
  52.5 13.2 %collective-permute-start.2 = (f32[192,512]{1,0:T(8,128)S(1)}, f32[192,512]{1,0:T(8,128)S(1)}, u32[]{:S(2)}, u32[]{:S(2)}) collective-permute-start(f32[192,512]{1,0:T(8,128)S(1)} %slice_bitcast_fusion.7), channel_id=1, source_target_pairs={{0,4},{4,8},{8,12},{12,16},{16,20},{20,24},{24,28},{28,0},{1,5},{5... | collective-permute-start | bytes 1179656 | tf_op jit(solution)/shard_map/ppermute | solution.py:13
  65.8 34.8 %copy-start.11 = (f32[192,384]{1,0:T(8,128)S(1)}, f32[192,384]{1,0:T(8,128)}, u32[]{:S(2)}) copy-start(f32[192,384]{1,0:T(8,128)} %param.9) | copy-start | bytes 884740
  66.6 1.4 copy-start.4
  68.0 34.2 %collective-permute-start.3 = (f32[192,512]{1,0:T(8,128)}, f32[192,512]{1,0:T(8,128)}, u32[]{:S(2)}, u32[]{:S(2)}) collective-permute-start(f32[192,512]{1,0:T(8,128)} %get-tuple-element.15), channel_id=1, source_target_pairs={{0,1},{1,2},{2,3},{3,0},{4,5},{5,6},{6,7},{7,4},{8,9},{9,10},{10,1... | collective-permute-start | bytes 1179656 | tf_op jit(solution)/shard_map/ppermute | solution.py:13
  104.1 3.9 %copy-start.2 = (f32[1,1,6,192,192]{4,3,2,1,0:T(8,128)S(1)}, f32[1,1,6,192,192]{4,3,2,1,0:T(8,128)}, u32[]{:S(2)}) copy-start(f32[1,1,6,192,192]{4,3,2,1,0:T(8,128)} %param.6) | copy-start | bytes 2654212
  122.8 1.8 %copy-start.3 = (f32[6,192,512]{2,1,0:T(8,128)}, f32[6,192,512]{2,1,0:T(8,128)S(1)}, u32[]{:S(2)}) copy-start(f32[6,192,512]{2,1,0:T(8,128)S(1)} %convolution_bitcast_fusion.1) | copy-start | bytes 7077892
  124.6 11.9 %collective-permute-start.4 = (f32[192,512]{1,0:T(8,128)}, f32[192,512]{1,0:T(8,128)}, u32[]{:S(2)}, u32[]{:S(2)}) collective-permute-start(f32[192,512]{1,0:T(8,128)} %get-tuple-element.7), channel_id=1, source_target_pairs={{0,28},{4,0},{8,4},{12,8},{16,12},{20,16},{24,20},{28,24},{1,29},{... | collective-permute-start | bytes 1179656 | tf_op jit(solution)/shard_map/ppermute | solution.py:13
  126.0 10.6 %collective-permute-start.5 = (f32[192,512]{1,0:T(8,128)}, f32[192,512]{1,0:T(8,128)}, u32[]{:S(2)}, u32[]{:S(2)}) collective-permute-start(f32[192,512]{1,0:T(8,128)} %get-tuple-element.9), channel_id=1, source_target_pairs={{0,3},{1,0},{2,1},{3,2},{4,7},{5,4},{6,5},{7,6},{8,11},{9,8},{10,9... | collective-permute-start | bytes 1179656 | tf_op jit(solution)/shard_map/ppermute | solution.py:13
  136.5 1.6 %copy-start.6 = (f32[1,192,512]{2,1,0:T(8,128)S(1)}, f32[1,192,512]{2,1,0:T(8,128)}, u32[]{:S(2)}) copy-start(f32[1,192,512]{2,1,0:T(8,128)} %get-tuple-element.8) | copy-start | bytes 1179652
Sparse Core Ops, SparseCore 0:
  102.4 32.0 all-reduce.1
where the time goes:
time: 148 us; the launch traced here: 147 us
  matrix products  36.1 us (24%)
  waiting for transfers between devices  33 us (22%)
  blocking collectives  32.6 us (22%)
  between operations  13.8 us (9%)
  local copies, waits for them, and re-layouts  13.2 us (9%)
  other arithmetic  9.77 us (7%)
  starting transfers between devices  8.85 us (6%)
    all_gather x1, blocking collectives, per_device(): lax.all_gather(restricted_residual, 'wide', axis=0, tiled=True)  32.6 us
    ppermute x6, waiting for transfers between devices, passed_along(): return lax.ppermute(value, axis, pairs)  24.5 us
    dot_general x4, matrix products, apply_faces(): jnp.einsum('fij,fjr->fir', blocks, fields, precision=exact_arithmetic_mode)  11.7 us
    dot_general x12, matrix products, newton_schulz(): jnp.einsum('bij,bjk->bik', matrices, approx, precision=exact_arithmetic_m...  8.92 us
    ppermute x6, starting transfers between devices, passed_along(): return lax.ppermute(value, axis, pairs)  8.85 us
    dot_general x12, matrix products, newton_schulz(): jnp.einsum('bij,bjk->bik', approx, product, precision=exact_arithmetic_mode)  8.59 us
    psum x1, waiting for transfers between devices, per_device(): summed = lax.psum(incomplete_total, 'narrow')  8.51 us
    unnamed x29, local copies, waits for them, and re-layouts  6.61 us
  transfers between devices with their start and end apart: 7, of which 4 were waited for; matrix products, arithmetic and copies ran while one was open for 18% of the time, Pallas kernels for 0%

commit v1 on v0

--- a/solution.py
+++ b/solution.py
@@ -5,6 +5,18 @@
 
 NS_STEPS = 12
 exact_arithmetic_mode = lax.Precision.HIGHEST
+
+
+def doubled_up(x, axis, dim):
+    ways, here = (lax.axis_size(axis), lax.axis_index(axis))
+    grown, reach = (x, 1)
+    while reach < ways:
+        theirs = lax.ppermute(grown, axis, [(d, d ^ reach) for d in range(ways)])
+        mine_first = jnp.concatenate([grown, theirs], axis=dim)
+        theirs_first = jnp.concatenate([theirs, grown], axis=dim)
+        grown = jnp.where(here & reach == 0, mine_first, theirs_first)
+        reach = 2 * reach
+    return grown
 
 
 def passed_along(value, axis, steps):
@@ -74,7 +86,7 @@
     restricted_residual = restricted_residual.reshape(-1, columns_count)
     incomplete_total = jnp.dot(
         coarse_inverse,
-        lax.all_gather(restricted_residual, "wide", axis=0, tiled=True),
+        doubled_up(restricted_residual, "wide", 0),
         precision=exact_arithmetic_mode,
         preferred_element_type=jnp.float32,
     )

time: 148 us -> 144 us (0.973)
  blocking collectives: 32.6 us -> 0 us
  starting transfers between devices: 8.85 us -> 26.1 us
  other arithmetic: 9.77 us -> 13.6 us
  waiting for transfers between devices: 33 us -> 36.8 us
  local copies, waits for them, and re-layouts: 13.2 us -> 16.2 us
    all_gather x1 -> x0, blocking collectives: 32.6 us -> none  [per_device(): lax.all_gather(restricted_residual, 'wide', axis=0, tiled=True)]
    ppermute x0 -> x3, waiting for transfers between devices: none -> 14.9 us  [doubled_up(): theirs = lax.ppermute(grown, axis, [(d, d ^ reach) for d in range(ways)])]
    ppermute x6, starting transfers between devices: 8.85 us -> 23.3 us  [passed_along(): return lax.ppermute(value, axis, pairs)]
    ppermute x6, waiting for transfers between devices: 24.5 us -> 15.3 us  [passed_along(): return lax.ppermute(value, axis, pairs)]
    ppermute x0 -> x3, starting transfers between devices: none -> 2.75 us  [doubled_up(): theirs = lax.ppermute(grown, axis, [(d, d ^ reach) for d in range(ways)])]
    unnamed x29 -> x23, local copies, waits for them, and re-layouts: 6.61 us -> 8.93 us
    psum x1, waiting for transfers between devices: 8.51 us -> 6.58 us  [per_device(): summed = lax.psum(incomplete_total, 'narrow')]
    select_n x0 -> x2, other arithmetic: none -> 1.85 us  [doubled_up(): grown = jnp.where(here & reach == 0, mine_first, theirs_first)]
  transfers between devices with their start and end apart: 7 -> 10, of which waited for: 4 -> 6; matrix products, arithmetic and copies ran while one was open for 18% -> 35% of each run, Pallas kernels for 0% -> 0%
where the time goes in v1:
time: 144 us
  matrix products  37.5 us (26%)
  waiting for transfers between devices  36.8 us (26%)
  starting transfers between devices  26.1 us (18%)
  local copies, waits for them, and re-layouts  16.2 us (11%)
  between operations  13.8 us (10%)
  other arithmetic  13.6 us (9%)
    ppermute x6, starting transfers between devices, passed_along(): return lax.ppermute(value, axis, pairs)  23.3 us
    ppermute x6, waiting for transfers between devices, passed_along(): return lax.ppermute(value, axis, pairs)  15.3 us
    ppermute x3, waiting for transfers between devices, doubled_up(): theirs = lax.ppermute(grown, axis, [(d, d ^ reach) for d in range(ways)])  14.9 us
    dot_general x4, matrix products, apply_faces(): jnp.einsum('fij,fjr->fir', blocks, fields, precision=exact_arithmetic_mode)  11.7 us
    dot_general x12, matrix products, newton_schulz(): jnp.einsum('bij,bjk->bik', matrices, approx, precision=exact_arithmetic_m...  8.95 us
    unnamed x23, local copies, waits for them, and re-layouts  8.93 us
    dot_general x12, matrix products, newton_schulz(): jnp.einsum('bij,bjk->bik', approx, product, precision=exact_arithmetic_mode)  8.57 us
    psum x1, waiting for transfers between devices, per_device(): summed = lax.psum(incomplete_total, 'narrow')  6.58 us
  transfers between devices with their start and end apart: 10, of which 6 were waited for; matrix products, arithmetic and copies ran while one was open for 35% of the time, Pallas kernels for 0%

profile of v1, /device:TPU:0, one launch (start us, length us, event | category | flops | bytes accessed | tf_op | source)
XLA Modules:
  0.0 143.9 jit_solution(17679067203004192778)
XLA Ops:
  6.5 1.4 add_bitcast_fusion.1
  8.0 2.2 %slice_bitcast_fusion.6 = (f32[192,512]{1,0:T(8,128)S(1)}, f32[192,512]{1,0:T(8,128)S(1)}, f32[1,192,512]{2,1,0:T(8,128)}) fusion(f32[1,1,6,192,512]{4,3,2,1,0:T(8,128)} %param.5), kind=kLoop, calls=%fused_computation.64 | loop fusion | flops 98304 | bytes 2752512 | tf_op jit(solution)/shard_map/squeeze | solution.py:48
  10.2 1.0 pad_maximum_fusion.4
  11.2 2.4 %collective-permute-start.1 = (f32[192,704]{1,0:T(8,128)}, f32[192,704]{1,0:T(8,128)S(1)}, u32[]{:S(2)}, u32[]{:S(2)}) collective-permute-start(f32[192,704]{1,0:T(8,128)} %pad_maximum_fusion.4), channel_id=1, source_target_pairs={{0,3},{1,0},{2,1},{3,2},{4,7},{5,4},{6,5},{7,6},{8,11},{9,8},{10,9... | collective-permute-start | bytes 1622024 | tf_op jit(solution)/shard_map/ppermute | solution.py:25
  14.7 4.6 %collective-permute-start = (f32[192,704]{1,0:T(8,128)}, f32[192,704]{1,0:T(8,128)}, u32[]{:S(2)}, u32[]{:S(2)}) collective-permute-start(f32[192,704]{1,0:T(8,128)} %pad_maximum_fusion.3), channel_id=1, source_target_pairs={{0,28},{4,0},{8,4},{12,8},{16,12},{20,16},{24,20},{28,24},{1,29},{... | collective-permute-start | bytes 1622024 | tf_op jit(solution)/shard_map/ppermute | solution.py:25
  19.2 2.1 %collective-permute-done.1 = f32[192,704]{1,0:T(8,128)S(1)} collective-permute-done((f32[192,704]{1,0:T(8,128)}, f32[192,704]{1,0:T(8,128)S(1)}, u32[]{:S(2)}, u32[]{:S(2)}) %collective-permute-start.1) | collective-permute-done | bytes 540704 | tf_op jit(solution)/shard_map/ppermute | solution.py:25
  22.2 9.6 %collective-permute-done = f32[192,704]{1,0:T(8,128)} collective-permute-done((f32[192,704]{1,0:T(8,128)}, f32[192,704]{1,0:T(8,128)}, u32[]{:S(2)}, u32[]{:S(2)}) %collective-permute-start) | collective-permute-done | bytes 540704 | tf_op jit(solution)/shard_map/ppermute | solution.py:25
  31.9 1.3 fusion.29
  33.5 1.7 %fusion.24 = (f32[1,192,512]{2,1,0:T(8,128)S(1)}, f32[1,192,512]{2,1,0:T(8,128)S(1)}) fusion(f32[192,704]{1,0:T(8,128)} %collective-permute-done, f32[1,1,6,192,512]{4,3,2,1,0:T(8,128)} %param.5, f32[192,704]{1,0:T(8,128)} %copy-done.8), kind=kLoop, calls=%fused_computation.58 | loop fusion | flops 196608 | bytes 2359296 | tf_op jit(solution)/shard_map/stack | solution.py:60
  54.1 1.2 fusion.10
  57.0 1.7 %collective-permute-start.2 = (f32[192,512]{1,0:T(8,128)}, f32[192,512]{1,0:T(8,128)}, u32[]{:S(2)}, u32[]{:S(2)}) collective-permute-start(f32[192,512]{1,0:T(8,128)} %slice_bitcast_fusion.7), channel_id=1, source_target_pairs={{0,4},{4,8},{8,12},{12,16},{16,20},{20,24},{24,28},{28,0},{1,5},{5... | collective-permute-start | bytes 1179656 | tf_op jit(solution)/shard_map/ppermute | solution.py:25
  58.8 5.7 %collective-permute-done.7 = f32[96,512]{1,0:T(8,128)} collective-permute-done((f32[96,512]{1,0:T(8,128)S(1)}, f32[96,512]{1,0:T(8,128)}, u32[]{:S(2)}, u32[]{:S(2)}) %collective-permute-start.7) | collective-permute-done | bytes 196640 | tf_op jit(solution)/shard_map/ppermute | solution.py:14
  64.6 1.8 %maximum_select_fusion.2 = f32[192,512]{1,0:T(8,128)} fusion(f32[96,512]{1,0:T(8,128)} %collective-permute-done.7, f32[96,512]{1,0:T(8,128)S(1)} %maximum_select_fusion.3, pred[]{:T(512)S(6)} %eq.10), kind=kLoop, calls=%fused_computation.59 | loop fusion | flops 294912 | bytes 786433 | tf_op jit(solution)/shard_map/jit(_where)/select_n | solution.py:17
  66.4 2.3 %collective-permute-start.8 = (f32[192,512]{1,0:T(8,128)}, f32[192,512]{1,0:T(8,128)}, u32[]{:S(2)}, u32[]{:S(2)}) collective-permute-start(f32[192,512]{1,0:T(8,128)} %maximum_select_fusion.2), channel_id=1, source_target_pairs={{0,16},{4,20},{8,24},{12,28},{16,0},{20,4},{24,8},{28,12},{1,17},{... | collective-permute-start | bytes 1179656 | tf_op jit(solution)/shard_map/ppermute | solution.py:14
  68.7 3.5 %collective-permute-done.2 = f32[192,512]{1,0:T(8,128)} collective-permute-done((f32[192,512]{1,0:T(8,128)}, f32[192,512]{1,0:T(8,128)}, u32[]{:S(2)}, u32[]{:S(2)}) %collective-permute-start.2) | collective-permute-done | bytes 393248 | tf_op jit(solution)/shard_map/ppermute | solution.py:25
  74.0 1.4 copy-done.5
  75.4 9.2 %collective-permute-done.8 = f32[192,512]{1,0:T(8,128)} collective-permute-done((f32[192,512]{1,0:T(8,128)}, f32[192,512]{1,0:T(8,128)}, u32[]{:S(2)}, u32[]{:S(2)}) %collective-permute-start.8) | collective-permute-done | bytes 393248 | tf_op jit(solution)/shard_map/ppermute | solution.py:14
  84.6 3.1 %convolution_bitcast_fusion.3 = f32[192,512]{1,0:T(8,128)} fusion(f32[192,384]{1,0:T(8,128)} %param.9, f32[192,512]{1,0:T(8,128)} %collective-permute-done.8, f32[192,512]{1,0:T(8,128)} %maximum_select_fusion.2, pred[]{:T(512)S(6)} %eq.9), kind=kOutput, calls=%fused_computation.19 | convolution fusion | flops 453574656 | bytes 1474561 | tf_op jit(solution)/shard_map/dot_general | solution.py:87
  87.7 1.8 %bitcast_dynamic-update-slice_fusion = f32[6,192,512]{2,1,0:T(8,128)} fusion(f32[6,192,512]{2,1,0:T(8,128)} %copy-done.5, f32[192,512]{1,0:T(8,128)} %collective-permute-done.3), kind=kLoop, calls=%fused_computation.60 | loop fusion | bytes 786432
  89.5 2.2 %slice_dynamic-update-slice_fusion = f32[6,192,512]{2,1,0:T(8,128)} fusion(f32[6,192,512]{2,1,0:T(8,128)} %bitcast_dynamic-update-slice_fusion, f32[3,192,512]{2,1,0:T(8,128)} %copy-done.1), kind=kLoop, calls=%fused_computation.30 | loop fusion | bytes 1572864
  91.6 1.8 %slice_dynamic-update-slice_fusion.1 = f32[6,192,512]{2,1,0:T(8,128)} fusion(f32[6,192,512]{2,1,0:T(8,128)} %slice_dynamic-update-slice_fusion, f32[3,192,512]{2,1,0:T(8,128)} %copy-done.1), kind=kLoop, calls=%fused_computation.53 | loop fusion | bytes 786432 | tf_op jit(solution)/shard_map/stack | solution.py:72
  93.4 4.0 %convolution_convert_fusion = bf16[6,512,192]{1,2,0:T(8,128)(2,1)S(1)} fusion(f32[6,192,512]{2,1,0:T(8,128)} %slice_dynamic-update-slice_fusion.1, f32[1,1,6,192,192]{4,3,2,1,0:T(8,128)S(1)} %copy-done.3), kind=kOutput, calls=%fused_computation.3 | convolution fusion | flops 1359544320 | bytes 4423680 | tf_op jit(solution)/shard_map/fij,fjr->fir/dot_general | solution.py:40
  97.4 3.4 %convolution_bitcast_fusion = f32[1152,512]{0,1:T(8,128)} fusion(bf16[1152,512]{1,0:T(8,128)(2,1)S(1)} %bitcast.126, bf16[1,1,1152,1152]{3,2,1,0:T(8,128)(2,1)S(1)} %copy-done), kind=kOutput, calls=%fused_computation | convolution fusion | flops 1358954496 | bytes 6193152 | tf_op jit(solution)/shard_map/dot_general | solution.py:98
  100.8 3.1 %copy.8 = f32[1152,512]{1,0:T(8,128)} copy(f32[1152,512]{0,1:T(8,128)} %convolution_bitcast_fusion) | data formatting | bytes 4718592 | tf_op jit(solution)/shard_map/dot_general | solution.py:98
  103.8 4.3 %convolution_bitcast_fusion.1 = f32[6,192,512]{2,1,0:T(8,128)S(1)} fusion(f32[6,192,512]{2,1,0:T(8,128)} %bitcast.125, f32[1,1,6,192,192]{4,3,2,1,0:T(8,128)} %param.6), kind=kOutput, calls=%fused_computation.2 | convolution fusion | flops 1358954496 | bytes 5603328 | tf_op jit(solution)/shard_map/fij,fjr->fir/dot_general | solution.py:40
  108.2 1.1 slice_bitcast_fusion.2
  110.0 11.9 %collective-permute-start.4 = (f32[192,512]{1,0:T(8,128)}, f32[192,512]{1,0:T(8,128)}, u32[]{:S(2)}, u32[]{:S(2)}) collective-permute-start(f32[192,512]{1,0:T(8,128)} %get-tuple-element.7), channel_id=1, source_target_pairs={{0,28},{4,0},{8,4},{12,8},{16,12},{20,16},{24,20},{28,24},{1,29},{... | collective-permute-start | bytes 1179656 | tf_op jit(solution)/shard_map/ppermute | solution.py:25
  121.9 2.8 %collective-permute-start.5 = (f32[192,512]{1,0:T(8,128)}, f32[192,512]{1,0:T(8,128)}, u32[]{:S(2)}, u32[]{:S(2)}) collective-permute-start(f32[192,512]{1,0:T(8,128)} %get-tuple-element.9), channel_id=1, source_target_pairs={{0,3},{1,0},{2,1},{3,2},{4,7},{5,4},{6,5},{7,6},{8,11},{9,8},{10,9... | collective-permute-start | bytes 1179656 | tf_op jit(solution)/shard_map/ppermute | solution.py:25
  124.7 6.6 %all-reduce.2.cloned.1.call-done = f32[192,512]{1,0:T(8,128)} async-done(((f32[192,512]{1,0:T(8,128)}), f32[192,512]{1,0:T(8,128)}) %all-reduce.2.cloned.1.call-update) | async-done | bytes 393232 | tf_op jit(solution)/shard_map/psum | solution.py:94
  132.1 1.1 convolution_bitcast_fusion.2
  133.3 1.5 %fusion.22 = (f32[1,192,512]{2,1,0:T(8,128)S(1)}, f32[1,192,512]{2,1,0:T(8,128)S(1)}) fusion(f32[192,512]{1,0:T(8,128)} %collective-permute-done.4, f32[6,192,512]{2,1,0:T(8,128)} %copy-done.4, f32[192,512]{1,0:T(8,128)} %collective-permute-done.5), kind=kLoop, calls=%fused_computation.52 | loop fusion | flops 196608 | bytes 2359296 | tf_op jit(solution)/shard_map/stack | solution.py:103
  134.8 2.2 %fusion.1 = f32[1,1,3,192,512]{4,3,2,1,0:T(8,128)} fusion(f32[3,192,512]{2,1,0:T(8,128)S(1)} %convolution_bitcast_fusion.2, f32[3,192,192]{2,1,0:T(8,128)S(1)} %convolution_subtract_fusion, f32[1,192,512]{2,1,0:T(8,128)S(1)} %copy-done.7, f32[1,192,512]{2,1,0:T(8,128)S(1)} %get-tuple-element.6, f32[1,192,512]{2,1,0:T(8,128)S(1)} %get-tuple-element.5), kind=kOutput, calls=%fused_computation.6 | convolution fusion | flops 680361984 | bytes 3981312 | tf_op jit(solution)/shard_map/fij,fjr->fir/dot_general | solution.py:40
  (62 shorter events, 26.1 us)
Async XLA Ops:
  6.5 90.8 %copy-start = (bf16[1,1,1152,1152]{3,2,1,0:T(8,128)(2,1)S(1)}, bf16[1,1,1152,1152]{3,2,1,0:T(8,128)(2,1)}, u32[]{:S(2)}) copy-start(bf16[1,1,1152,1152]{3,2,1,0:T(8,128)(2,1)} %param.7) | copy-start | bytes 7962628
  6.5 124.7 %all-reduce.2.cloned.1.call-start = ((), (), s32[]{:S(2)}) async-start(), calls=%async_computation | async-start | bytes 786432 | tf_op jit(solution)/shard_map/psum | solution.py:94
  11.2 10.1 %collective-permute-start.1 = (f32[192,704]{1,0:T(8,128)}, f32[192,704]{1,0:T(8,128)S(1)}, u32[]{:S(2)}, u32[]{:S(2)}) collective-permute-start(f32[192,704]{1,0:T(8,128)} %pad_maximum_fusion.4), channel_id=1, source_target_pairs={{0,3},{1,0},{2,1},{3,2},{4,7},{5,4},{6,5},{7,6},{8,11},{9,8},{10,9... | collective-permute-start | bytes 1622024 | tf_op jit(solution)/shard_map/ppermute | solution.py:25
  14.7 17.2 %collective-permute-start = (f32[192,704]{1,0:T(8,128)}, f32[192,704]{1,0:T(8,128)}, u32[]{:S(2)}, u32[]{:S(2)}) collective-permute-start(f32[192,704]{1,0:T(8,128)} %pad_maximum_fusion.3), channel_id=1, source_target_pairs={{0,28},{4,0},{8,4},{12,8},{16,12},{20,16},{24,20},{28,24},{1,29},{... | collective-permute-start | bytes 1622024 | tf_op jit(solution)/shard_map/ppermute | solution.py:25
  21.4 0.8 copy-start.8
  33.4 1.8 %copy-start.6 = (f32[1,192,512]{2,1,0:T(8,128)S(1)}, f32[1,192,512]{2,1,0:T(8,128)}, u32[]{:S(2)}) copy-start(f32[1,192,512]{2,1,0:T(8,128)} %get-tuple-element.14) | copy-start | bytes 1179652
  33.5 1.8 %copy-start.9 = (f32[3,192,16]{1,2,0:T(8,128)S(1)}, f32[3,192,16]{1,2,0:T(8,128)}, u32[]{:S(2)}) copy-start(f32[3,192,16]{1,2,0:T(8,128)} %param.8) | copy-start | bytes 110596
  36.0 22.8 %collective-permute-start.6 = (f32[48,512]{1,0:T(8,128)S(1)}, f32[48,512]{1,0:T(8,128)S(1)}, u32[]{:S(2)}, u32[]{:S(2)}) collective-permute-start(f32[48,512]{1,0:T(8,128)S(1)} %bitcast.128), channel_id=1, source_target_pairs={{0,4},{4,0},{8,12},{12,8},{16,20},{20,16},{24,28},{28,24},{1,5},{5... | collective-permute-start | bytes 294920 | tf_op jit(solution)/shard_map/ppermute | solution.py:14
  55.2 1.0 copy-start.1
  57.0 15.1 %collective-permute-start.2 = (f32[192,512]{1,0:T(8,128)}, f32[192,512]{1,0:T(8,128)}, u32[]{:S(2)}, u32[]{:S(2)}) collective-permute-start(f32[192,512]{1,0:T(8,128)} %slice_bitcast_fusion.7), channel_id=1, source_target_pairs={{0,4},{4,8},{8,12},{12,16},{16,20},{20,24},{24,28},{28,0},{1,5},{5... | collective-permute-start | bytes 1179656 | tf_op jit(solution)/shard_map/ppermute | solution.py:25
  58.7 5.8 %collective-permute-start.7 = (f32[96,512]{1,0:T(8,128)S(1)}, f32[96,512]{1,0:T(8,128)}, u32[]{:S(2)}, u32[]{:S(2)}) collective-permute-start(f32[96,512]{1,0:T(8,128)S(1)} %maximum_select_fusion.3), channel_id=1, source_target_pairs={{0,8},{4,12},{8,0},{12,4},{16,24},{20,28},{24,16},{28,20},{1,9},{5... | collective-permute-start | bytes 589832 | tf_op jit(solution)/shard_map/ppermute | solution.py:14
  58.8 14.4 %copy-start.2 = (f32[3,192,512]{2,1,0:T(8,128)S(1)}, f32[3,192,512]{2,1,0:T(8,128)}, u32[]{:S(2)}) copy-start(f32[3,192,512]{2,1,0:T(8,128)} %copy-done.1) | copy-start | bytes 3538948
  66.4 18.2 %collective-permute-start.8 = (f32[192,512]{1,0:T(8,128)}, f32[192,512]{1,0:T(8,128)}, u32[]{:S(2)}, u32[]{:S(2)}) collective-permute-start(f32[192,512]{1,0:T(8,128)} %maximum_select_fusion.2), channel_id=1, source_target_pairs={{0,16},{4,20},{8,24},{12,28},{16,0},{20,4},{24,8},{28,12},{1,17},{... | collective-permute-start | bytes 1179656 | tf_op jit(solution)/shard_map/ppermute | solution.py:14
  74.0 1.4 copy-start.5
  75.4 12.2 %collective-permute-start.3 = (f32[192,512]{1,0:T(8,128)}, f32[192,512]{1,0:T(8,128)}, u32[]{:S(2)}, u32[]{:S(2)}) collective-permute-start(f32[192,512]{1,0:T(8,128)} %get-tuple-element.15), channel_id=1, source_target_pairs={{0,1},{1,2},{2,3},{3,0},{4,5},{5,6},{6,7},{7,4},{8,9},{9,10},{10,1... | collective-permute-start | bytes 1179656 | tf_op jit(solution)/shard_map/ppermute | solution.py:25
  89.4 3.9 %copy-start.3 = (f32[1,1,6,192,192]{4,3,2,1,0:T(8,128)S(1)}, f32[1,1,6,192,192]{4,3,2,1,0:T(8,128)}, u32[]{:S(2)}) copy-start(f32[1,1,6,192,192]{4,3,2,1,0:T(8,128)} %param.6) | copy-start | bytes 2654212
  108.2 1.8 %copy-start.4 = (f32[6,192,512]{2,1,0:T(8,128)}, f32[6,192,512]{2,1,0:T(8,128)S(1)}, u32[]{:S(2)}) copy-start(f32[6,192,512]{2,1,0:T(8,128)S(1)} %convolution_bitcast_fusion.1) | copy-start | bytes 7077892
  110.0 23.3 %collective-permute-start.4 = (f32[192,512]{1,0:T(8,128)}, f32[192,512]{1,0:T(8,128)}, u32[]{:S(2)}, u32[]{:S(2)}) collective-permute-start(f32[192,512]{1,0:T(8,128)} %get-tuple-element.7), channel_id=1, source_target_pairs={{0,28},{4,0},{8,4},{12,8},{16,12},{20,16},{24,20},{28,24},{1,29},{... | collective-permute-start | bytes 1179656 | tf_op jit(solution)/shard_map/ppermute | solution.py:25
  121.9 11.4 %collective-permute-start.5 = (f32[192,512]{1,0:T(8,128)}, f32[192,512]{1,0:T(8,128)}, u32[]{:S(2)}, u32[]{:S(2)}) collective-permute-start(f32[192,512]{1,0:T(8,128)} %get-tuple-element.9), channel_id=1, source_target_pairs={{0,3},{1,0},{2,1},{3,2},{4,7},{5,4},{6,5},{7,6},{8,11},{9,8},{10,9... | collective-permute-start | bytes 1179656 | tf_op jit(solution)/shard_map/ppermute | solution.py:25
  133.3 1.6 %copy-start.7 = (f32[1,192,512]{2,1,0:T(8,128)S(1)}, f32[1,192,512]{2,1,0:T(8,128)}, u32[]{:S(2)}) copy-start(f32[1,192,512]{2,1,0:T(8,128)} %get-tuple-element.8) | copy-start | bytes 1179652
Sparse Core Ops, SparseCore 0:
  87.8 43.4 all-reduce.1
